TPU v7x, 256 devices: a whole 4x4x8 slice. The times are simulated.
256 devices in a mesh: tm: 16 (over y_hi, z), sub: 16 (over x, y_lo, core).
Axes of the slice: x: 4, y: 4 (y_hi: 2, y_lo: 2; y = y_hi * 2 + y_lo), z: 8, core: 2. Of those that a mesh axis runs over, the one named last changes fastest.
Arguments:
- frames: bfloat16 [16384, 1024], P(('tm', 'sub')), may hold values from -16 to 16
- modulation: float32 [8, 1024], replicated, may hold values from -4 to 4
- w_project: bfloat16 [3, 1024, 1024], P(None, None, 'sub'), may hold values from -1 to 1
- w_heads_out: bfloat16 [1024, 1024], P('sub'), may hold values from -0.25 to 0.25
- w_up: bfloat16 [1024, 4096], P(None, 'sub'), may hold values from -0.1875 to 0.1875
- w_down: bfloat16 [4096, 1024], P('sub'), may hold values from -0.125 to 0.125
- w_velocity: bfloat16 [1024, 100], replicated, may hold values from -0.1875 to 0.1875
- noisy_mel: float32 [16384, 100], P('tm'), may hold values from -6 to 6
- w_prelude: bfloat16 [7, 1536, 100], P(None, 'sub'), may hold values from -0.21875 to 0.21875
- w_upsample: bfloat16 [8, 1536, 768], P(None, 'sub'), may hold values from -0.109375 to 0.109375
- snake_alpha: float32 [2, 768], replicated, may hold values from 0.3 to 3
- w_dilated: bfloat16 [3, 768, 768], P(None, 'sub'), may hold values from -0.125 to 0.125
- w_plain: bfloat16 [3, 768, 768], P(None, 'sub'), may hold values from -0.125 to 0.125
Outputs:
- mel_next: float32 [16384, 100], P('tm')
- section_out: bfloat16 [65536, 768], P(('tm', 'sub'))
All inputs are finite; a program needn't handle non-finite values.
Results may differ from a plain program's by a relative error of at most 0.03.
Values may be sent and summed in bfloat16 or wider, within the bound.
No kernel may reach another device: no remote copies, remote signals or barrier semaphores. Data moves between devices by JAX's collectives and lax.ppermute only.
A program may use at most 64 MiB of HBM per device.

v0:
```python
import math
import jax
import jax.numpy as jnp
from jax import lax
from jax.sharding import PartitionSpec as P

HEAD_DIM = 64
BLK = 256
epsilon = 1e-06


def from_behind(block, axis, distance):
    devices = range(lax.axis_size(axis))
    route = [(i - distance, i) for i in devices if i - distance in devices]
    return lax.ppermute(block, axis, route)


def extended_2(cells, sides, width):
    for axis, dim in sides:
        count = lax.axis_size(axis)
        ends = count - 1
        head = lax.slice_in_dim(cells, 0, width, axis=dim)
        tail = lax.slice_in_dim(cells, cells.shape[dim] - width, cells.shape[dim], axis=dim)
        cells = jnp.concatenate(
            [
                lax.ppermute(tail, axis, [(i, (i + 1) % count) for i in range(ends)]),
                cells,
                lax.ppermute(head, axis, [((i + 1) % count, i) for i in range(ends)]),
            ],
            axis=dim,
        )
    return cells


def norm_rows(rows, offset_row, scale_row):
    rows = rows.astype(jnp.float32)
    center = jnp.mean(rows, axis=-1, keepdims=True)
    square = jnp.mean(rows * rows, axis=-1, keepdims=True)
    spread = square - center * center
    return (rows - center) * lax.rsqrt(spread + epsilon) * (1.0 + scale_row) + offset_row


def snake_act(values, alpha_row):
    return values + jnp.square(jnp.sin(alpha_row * values)) / alpha_row


def contract_first(left, right):
    return lax.dot_general(
        left, right, (((0,), (0,)), ((), ())), preferred_element_type=jnp.float32
    )


def phase_terms(prelude_cols, tap_weights, first_frame, span):
    current = lax.dynamic_slice_in_dim(prelude_cols, 1, span, 1)
    earlier = lax.dynamic_slice_in_dim(prelude_cols, first_frame, span, 1)
    later_frames = lax.dynamic_slice_in_dim(prelude_cols, 2, span, 1)

    def tap_product(source, offset):
        return contract_first(source, tap_weights[offset])

    phases = jnp.stack(
        [
            tap_product(current, 2) + tap_product(earlier, 6),
            tap_product(current, 3) + tap_product(earlier, 7),
            tap_product(current, 4) + tap_product(later_frames, 0),
            tap_product(current, 5) + tap_product(later_frames, 1),
        ],
        1,
    )
    return phases.reshape((4 * span, phases.shape[2]))


def block_attention(queries, keys_now, values_now, lookback, is_first):
    frame_count = queries.shape[0]
    head_count = queries.shape[1] // HEAD_DIM
    blocks = frame_count // BLK
    block_shape = (blocks, BLK, head_count, HEAD_DIM)
    edge_shape = (1, BLK, head_count, HEAD_DIM)
    key_blocks = keys_now.reshape(block_shape)
    value_blocks = values_now.reshape(block_shape)
    key_all = jnp.concatenate(
        [jnp.concatenate([lookback[0].reshape(edge_shape), key_blocks[:-1]], 0), key_blocks], 1
    )
    value_all = jnp.concatenate(
        [jnp.concatenate([lookback[1].reshape(edge_shape), value_blocks[:-1]], 0), value_blocks], 1
    )
    scores = jnp.einsum(
        "bqhd,bkhd->bhqk", queries.reshape(block_shape), key_all, preferred_element_type=jnp.float32
    ) / math.sqrt(HEAD_DIM)
    block_ids = lax.broadcasted_iota(jnp.int32, (blocks, 1, 1, 2 * BLK), 0)
    key_ids = lax.broadcasted_iota(jnp.int32, (blocks, 1, 1, 2 * BLK), 3)
    allowed = (block_ids > 0) | (key_ids >= BLK) | jnp.logical_not(is_first)
    scores = jnp.where(allowed, scores, -1e30)
    largest = jnp.max(scores, axis=-1, keepdims=True)
    raised = jnp.exp(scores - largest)
    weights = (raised / jnp.sum(raised, axis=-1, keepdims=True)).astype(jnp.bfloat16)
    attended = jnp.einsum("bhqk,bkhd->bqhd", weights, value_all, preferred_element_type=jnp.float32)
    return attended.reshape((frame_count, head_count * HEAD_DIM)).astype(jnp.bfloat16)


def dilated_conv(extended, row_count, w_dilated):
    empty_sum = jnp.zeros((row_count, w_dilated.shape[2]), jnp.float32)
    running = empty_sum
    weight_rows = lax.all_gather(w_dilated, "sub", axis=1, tiled=True)
    for offset in range(3):
        running = running + jnp.dot(
            extended[3 * offset : 3 * offset + row_count],
            weight_rows[offset],
            preferred_element_type=jnp.float32,
        )
    return running


def plain_conv(extended, row_count, w_plain):
    empty_sum = jnp.zeros((row_count, w_plain.shape[2]), jnp.float32)
    running = empty_sum
    weight_rows = lax.all_gather(w_plain, "sub", axis=1, tiled=True)
    for offset in range(3):
        running = running + jnp.dot(
            extended[offset : offset + row_count],
            weight_rows[offset],
            preferred_element_type=jnp.float32,
        )
    return running


def body(
    frames,
    modulation,
    w_project,
    w_heads_out,
    w_up,
    w_down,
    w_velocity,
    noisy_mel,
    w_prelude,
    w_upsample,
    snake_alpha,
    w_dilated,
    w_plain,
):
    own_rows = frames.shape[0]
    sub_index = lax.axis_index("sub")
    time_index = lax.axis_index("tm")
    gathered = lax.all_gather(frames, "sub", axis=0, tiled=True)
    frame_count = gathered.shape[0]
    first_norm = norm_rows(gathered, modulation[0], modulation[1]).astype(jnp.bfloat16)
    projected = jnp.einsum(
        "td,kde->kte", first_norm, w_project, preferred_element_type=jnp.float32
    ).astype(jnp.bfloat16)
    lookback = from_behind(
        (projected[1, frame_count - BLK :], projected[2, frame_count - BLK :]), "tm", 1
    )
    heads_out = block_attention(projected[0], projected[1], projected[2], lookback, time_index == 0)
    attn = lax.psum_scatter(
        jnp.dot(heads_out, w_heads_out, preferred_element_type=jnp.float32).astype(jnp.bfloat16),
        "sub",
        scatter_dimension=0,
        tiled=True,
    ).astype(jnp.float32)
    mixed_rows = (frames.astype(jnp.float32) + modulation[2] * attn).astype(jnp.bfloat16)
    own_norm = norm_rows(mixed_rows, modulation[3], modulation[4]).astype(jnp.bfloat16)
    second_norm = lax.all_gather(own_norm, "sub", axis=0, tiled=True)
    hidden = jax.nn.gelu(
        jnp.dot(second_norm, w_up, preferred_element_type=jnp.float32), approximate=True
    ).astype(jnp.bfloat16)
    feed = lax.psum_scatter(
        jnp.dot(hidden, w_down, preferred_element_type=jnp.float32).astype(jnp.bfloat16),
        "sub",
        scatter_dimension=0,
        tiled=True,
    ).astype(jnp.float32)
    final_rows = (mixed_rows.astype(jnp.float32) + modulation[5] * feed).astype(jnp.bfloat16)
    final_norm = norm_rows(final_rows, modulation[6], modulation[7]).astype(jnp.bfloat16)
    velocity = jnp.dot(final_norm, w_velocity, preferred_element_type=jnp.float32)
    noisy_own = lax.dynamic_slice_in_dim(noisy_mel, sub_index * own_rows, own_rows, 0)
    mel_own = noisy_own + 0.5 * velocity
    mel_next = lax.all_gather(mel_own, "sub", axis=0, tiled=True)
    mel_low = mel_next.astype(jnp.bfloat16)
    mel_wide = extended_2(mel_low, (("tm", 0),), 4)
    columns = frame_count + 2
    prelude = jnp.zeros((w_prelude.shape[1], columns), jnp.float32)
    for offset in range(7):
        prelude = prelude + lax.dot_general(
            w_prelude[offset],
            mel_wide[offset : offset + columns],
            (((1,), (1,)), ((), ())),
            preferred_element_type=jnp.float32,
        )
    frame_pos = time_index * frame_count - 1 + lax.broadcasted_iota(jnp.int32, (1, columns), 1)
    inside = (frame_pos >= 0) & (frame_pos < lax.axis_size("tm") * frame_count)
    prelude = jnp.where(inside, prelude, 0.0).astype(jnp.bfloat16)
    samples_dev = 4 * own_rows
    up_x = lax.psum_scatter(
        phase_terms(
            prelude, w_upsample, jnp.int32(0) // 4, samples_dev * lax.axis_size("sub") // 4
        ).astype(jnp.bfloat16),
        "sub",
        scatter_dimension=0,
        tiled=True,
    )
    act_one = snake_act(up_x.astype(jnp.float32), snake_alpha[0]).astype(jnp.bfloat16)
    wide_one = extended_2(act_one, ((("tm", "sub"), 0),), 3)
    inner_conv = dilated_conv(wide_one, samples_dev, w_dilated)
    act_two = snake_act(inner_conv, snake_alpha[1]).astype(jnp.bfloat16)
    wide_two = extended_2(act_two, ((("tm", "sub"), 0),), 1)
    outer_conv = plain_conv(wide_two, samples_dev, w_plain)
    section_out = (up_x.astype(jnp.float32) + outer_conv).astype(jnp.bfloat16)
    return (mel_next, section_out)


def solution(mesh):
    in_specs = (
        P(("tm", "sub"), None),
        P(),
        P(None, None, "sub"),
        P("sub", None),
        P(None, "sub"),
        P("sub", None),
        P(),
        P("tm", None),
        P(None, "sub", None),
        P(None, "sub", None),
        P(),
        P(None, "sub", None),
        P(None, "sub", None),
    )
    out_specs = (P("tm", None), P(("tm", "sub"), None))
    return jax.shard_map(body, mesh=mesh, in_specs=in_specs, out_specs=out_specs, check_vma=False)
```

profile of v0, /device:TPU:1, one launch (start us, length us, event | category | flops | bytes accessed | tf_op | source)
XLA Modules:
  0.0 477.0 jit_solution(3565787769455806827)
XLA Ops:
  7.2 0.7 all-gather.5.cloned.1.call-update
  8.0 0.1 or_or_fusion
  8.1 1.1 slice_add_fusion
  9.2 41.1 %all-gather.5.cloned.1.call-done = bf16[1024,1024]{1,0:T(8,128)(2,1)} async-done(((bf16[64,1024]{1,0:T(8,128)(2,1)}), bf16[1024,1024]{1,0:T(8,128)(2,1)}) %all-gather.5.cloned.1.call-update) | async-done | bytes 2097168 | tf_op jit(solution)/shard_map/all_gather | solution.py:145
  50.2 2.4 convert_reduce_fusion
  52.7 2.2 fusion.14
  55.0 3.2 collective-permute-start.1
  58.6 3.2 collective-permute-start
  61.8 2.2 fusion.181
  64.0 2.1 fusion.29
  66.1 0.1 copy.32
  66.3 2.1 convolution_convert_fusion.1
  68.5 64.6 %reduce-scatter.4.cloned.1.call-done = bf16[64,1024]{1,0:T(8,128)(2,1)} async-done(((bf16[1024,1024]{1,0:T(8,128)(2,1)}), bf16[64,1024]{1,0:T(8,128)(2,1)}) %reduce-scatter.4.cloned.1.call-update) | async-done | bytes 131088 | tf_op jit(solution)/shard_map/reduce_scatter | solution.py:155
  133.1 1.1 convert_reduce_fusion.1
  134.2 0.8 fusion.84
  135.0 38.8 %all-gather.7.cloned.1.call-done = bf16[1024,1024]{1,0:T(8,128)(2,1)} async-done(((bf16[64,1024]{1,0:T(8,128)(2,1)}), bf16[1024,1024]{1,0:T(8,128)(2,1)}) %all-gather.7.cloned.1.call-update) | async-done | bytes 2097168 | tf_op jit(solution)/shard_map/all_gather | solution.py:163
  173.8 5.2 %convolution_convert_fusion = bf16[1024,1024]{1,0:T(8,128)(2,1)} fusion(bf16[256,1024]{1,0:T(8,128)(2,1)S(1)} %copy-done, bf16[1024,1024]{1,0:T(8,128)(2,1)} %all-gather.7.cloned.1.call-done, bf16[1024,256]{1,0:T(8,128)(2,1)S(1)} %copy-done.11), kind=kOutput, calls=%fused_computation.27 | convolution fusion | flops 1077149696 | bytes 5242880 | tf_op jit(solution)/shard_map/dot_general | solution.py:168
  179.1 1.0 constant_dynamic-slice_fusion
  180.1 62.5 %reduce-scatter.6.cloned.1.call-done = bf16[64,1024]{1,0:T(8,128)(2,1)} async-done(((bf16[1024,1024]{1,0:T(8,128)(2,1)}), bf16[64,1024]{1,0:T(8,128)(2,1)}) %reduce-scatter.6.cloned.1.call-update) | async-done | bytes 131088 | tf_op jit(solution)/shard_map/reduce_scatter | solution.py:167
  242.6 1.1 convert_reduce_fusion.2
  243.7 0.2 fusion.30
  244.0 21.4 %all_gather.17 = f32[1024,100]{1,0:T(8,128)S(1)} all-gather(f32[64,100]{1,0:T(8,128)S(1)} %fusion.30), channel_id=1, replica_groups=mesh['tm'=16,'sub'=16] {'sub'}, dimensions={0}, use_global_device_ids=true | all-gather | bytes 435200 | tf_op jit(solution)/shard_map/all_gather | solution.py:178
  265.4 0.8 copy-done.2
  266.2 3.2 collective-permute-start.2
  269.5 1.5 collective-permute-start.3
  271.0 2.8 collective-permute-done.3
  273.8 0.7 concatenate.44
  274.5 0.2 fusion.70
  274.7 0.2 fusion.62
  275.0 0.2 fusion.72
  275.2 0.2 fusion.59
  275.5 0.2 fusion.56
  275.7 0.2 fusion.66
  276.0 0.3 fusion.13
  276.3 0.7 copy-done.6
  277.0 0.7 fusion.114
  277.7 0.7 fusion.111
  278.4 0.7 fusion.108
  279.2 0.7 fusion.105
  279.9 0.6 fusion.17
  280.5 0.6 fusion.18
  281.1 0.7 fusion.19
  281.9 0.7 fusion.20
  282.6 0.8 pad_maximum_fusion
  283.4 7.5 %copy.33 = bf16[1024,4,768]{2,1,0:T(4,128)(2,1)} copy(bf16[1024,4,768]{2,0,1:T(8,128)(2,1)S(1)} %pad_maximum_fusion) | data formatting | bytes 12582912 | tf_op jit(solution)/shard_map/stack | solution.py:61
  290.9 10.7 %convert_element_type.111 = bf16[4096,768]{1,0:T(8,128)(2,1)} reshape(bf16[1024,4,768]{2,1,0:T(4,128)(2,1)} %copy.33) | data formatting | bytes 12582912 | tf_op jit(solution)/shard_map/convert_element_type | solution.py:197
  301.7 0.5 all-gather.9.cloned.1.call-update
  302.3 0.3 all-gather.11.cloned.1.call-start
  302.5 0.5 all-gather.11.cloned.1.call-update
  303.1 1.0 copy.34
  304.0 78.0 %reduce-scatter.8.cloned.1.call-done = bf16[256,768]{1,0:T(8,128)(2,1)} async-done(((bf16[4096,768]{1,0:T(8,128)(2,1)}), bf16[256,768]{1,0:T(8,128)(2,1)}) %reduce-scatter.8.cloned.1.call-update) | async-done | bytes 393232 | tf_op jit(solution)/shard_map/reduce_scatter | solution.py:194
  382.1 3.6 fusion.45
  385.7 1.9 collective-permute-start.5
  387.7 3.6 collective-permute-start.4
  391.3 32.0 %all-gather.9.cloned.1.call-done = bf16[3,768,768]{2,1,0:T(8,128)(2,1)} async-done(((bf16[3,48,768]{2,1,0:T(8,128)(2,1)}), bf16[3,768,768]{2,1,0:T(8,128)(2,1)}) %all-gather.9.cloned.1.call-update) | async-done | bytes 3538960 | tf_op jit(solution)/shard_map/all_gather | solution.py:104
  423.3 1.7 fusion.28
  425.0 1.8 fusion.27
  426.8 4.2 add_convert_fusion.4
  431.1 2.2 collective-permute-start.7
  433.3 3.5 collective-permute-start.6
  436.8 27.2 %all-gather.11.cloned.1.call-done = bf16[3,768,768]{2,1,0:T(8,128)(2,1)} async-done(((bf16[3,48,768]{2,1,0:T(8,128)(2,1)}), bf16[3,768,768]{2,1,0:T(8,128)(2,1)}) %all-gather.11.cloned.1.call-update) | async-done | bytes 3538960 | tf_op jit(solution)/shard_map/all_gather | solution.py:117
  464.0 1.7 fusion.26
  465.8 1.8 fusion.25
  467.6 2.5 fusion.24
  (67 shorter events, 1.1 us)
Async XLA Ops:
  7.2 166.6 %copy-start = (bf16[256,1024]{1,0:T(8,128)(2,1)S(1)}, bf16[256,1024]{1,0:T(8,128)(2,1)}, u32[]{:S(2)}) copy-start(bf16[256,1024]{1,0:T(8,128)(2,1)} %param.18) | copy-start | bytes 1572868
  7.2 43.1 %all-gather.5.cloned.1.call-start = ((), (), s32[]{:S(2)}) async-start(), calls=%async_computation.3 | async-start | bytes 2228224 | tf_op jit(solution)/shard_map/all_gather | solution.py:145
  7.9 125.2 %reduce-scatter.4.cloned.1.call-start = ((), (), s32[]{:S(2)}) async-start(), calls=%async_computation.4 | async-start | bytes 2228224 | tf_op jit(solution)/shard_map/reduce_scatter | solution.py:155
  50.2 2.4 copy-start.4
  55.0 6.8 %collective-permute-start.1 = (bf16[256,64]{0,1:T(8,128)(2,1)S(1)}, bf16[256,64]{0,1:T(8,128)(2,1)S(1)}, u32[]{:S(2)}, u32[]{:S(2)}) collective-permute-start(bf16[256,64]{0,1:T(8,128)(2,1)S(1)} %get-tuple-element.21), channel_id=1, source_target_pairs={{0,16},{16,32},{32,48},{48,64},{64,80},{80,96},{96,112},{112,128},... | collective-permute-start | bytes 98312 | tf_op jit(solution)/shard_map/ppermute | solution.py:15
  58.6 5.4 %collective-permute-start = (bf16[256,64]{0,1:T(8,128)(2,1)S(1)}, bf16[256,64]{0,1:T(8,128)(2,1)S(1)}, u32[]{:S(2)}, u32[]{:S(2)}) collective-permute-start(bf16[256,64]{0,1:T(8,128)(2,1)S(1)} %get-tuple-element.20), channel_id=1, source_target_pairs={{0,16},{16,32},{32,48},{48,64},{64,80},{80,96},{96,112},{112,128},... | collective-permute-start | bytes 98312 | tf_op jit(solution)/shard_map/ppermute | solution.py:15
  64.0 2.3 copy-start.9
  66.3 66.8 %copy-start.7 = (bf16[64,1024]{1,0:T(8,128)(2,1)S(1)}, bf16[64,1024]{1,0:T(8,128)(2,1)}, u32[]{:S(2)}) copy-start(bf16[64,1024]{1,0:T(8,128)(2,1)} %param.13) | copy-start | bytes 393220
  66.3 107.5 %copy-start.11 = (bf16[1024,256]{1,0:T(8,128)(2,1)S(1)}, bf16[1024,256]{1,0:T(8,128)(2,1)}, u32[]{:S(2)}) copy-start(bf16[1024,256]{1,0:T(8,128)(2,1)} %param.17) | copy-start | bytes 1572868
  68.4 105.4 %all-gather.7.cloned.1.call-start = ((), (), s32[]{:S(2)}) async-start(), calls=%async_computation.5 | async-start | bytes 2228224 | tf_op jit(solution)/shard_map/all_gather | solution.py:163
  135.0 107.7 %reduce-scatter.6.cloned.1.call-start = ((), (), s32[]{:S(2)}) async-start(), calls=%async_computation.6 | async-start | bytes 2228224 | tf_op jit(solution)/shard_map/reduce_scatter | solution.py:167
  179.0 64.7 %copy-start.12 = (bf16[1024,100]{0,1:T(8,128)(2,1)S(1)}, bf16[1024,100]{0,1:T(8,128)(2,1)}, u32[]{:S(2)}) copy-start(bf16[1024,100]{0,1:T(8,128)(2,1)} %param.19) | copy-start | bytes 614404
  179.0 95.5 %copy-start.8 = (bf16[7,96,100]{2,1,0:T(8,128)(2,1)S(1)}, bf16[7,96,100]{2,1,0:T(8,128)(2,1)}, u32[]{:S(2)}) copy-start(bf16[7,96,100]{2,1,0:T(8,128)(2,1)} %param.21) | copy-start | bytes 403204
  179.0 203.1 %reduce-scatter.8.cloned.1.call-start = ((), (), s32[]{:S(2)}) async-start(), calls=%async_computation.7 | async-start | bytes 6684672 | tf_op jit(solution)/shard_map/reduce_scatter | solution.py:194
  265.4 0.8 copy-start.2
  266.2 4.7 collective-permute-start.2
  269.5 4.3 collective-permute-start.3
  275.7 1.3 copy-start.6
  301.7 1.4 copy-start.10
  301.7 1.4 copy-start.3
  301.7 121.6 %all-gather.9.cloned.1.call-start = ((), (), s32[]{:S(2)}) async-start(), calls=%async_computation.8 | async-start | bytes 3760128 | tf_op jit(solution)/shard_map/all_gather | solution.py:104
  302.3 161.7 %all-gather.11.cloned.1.call-start = ((), (), s32[]{:S(2)}) async-start(), calls=%async_computation.9 | async-start | bytes 3760128 | tf_op jit(solution)/shard_map/all_gather | solution.py:117
  385.7 39.3 %collective-permute-start.5 = (bf16[3,768]{1,0:T(4,128)(2,1)S(1)}, bf16[3,768]{1,0:T(4,128)(2,1)S(1)}, u32[]{:S(2)}, u32[]{:S(2)}) collective-permute-start(bf16[3,768]{1,0:T(4,128)(2,1)S(1)} %get-tuple-element.19), channel_id=1, source_target_pairs={{1,0},{2,1},{3,2},{4,3},{5,4},{6,5},{7,6},{8,7},{9,8},{10,9},{11,1... | collective-permute-start | bytes 13832 | tf_op jit(solution)/shard_map/ppermute | solution.py:28
  387.7 39.1 %collective-permute-start.4 = (bf16[3,768]{1,0:T(4,128)(2,1)S(1)}, bf16[3,768]{1,0:T(4,128)(2,1)S(1)}, u32[]{:S(2)}, u32[]{:S(2)}) collective-permute-start(bf16[3,768]{1,0:T(4,128)(2,1)S(1)} %get-tuple-element.18), channel_id=1, source_target_pairs={{0,1},{1,2},{2,3},{3,4},{4,5},{5,6},{6,7},{7,8},{8,9},{9,10},{10,1... | collective-permute-start | bytes 13832 | tf_op jit(solution)/shard_map/ppermute | solution.py:26
  431.1 34.7 %collective-permute-start.7 = (bf16[1,768]{1,0:T(2,128)(2,1)S(1)}, bf16[1,768]{1,0:T(2,128)(2,1)S(1)}, u32[]{:S(2)}, u32[]{:S(2)}) collective-permute-start(bf16[1,768]{1,0:T(2,128)(2,1)S(1)} %get-tuple-element.17), channel_id=1, source_target_pairs={{1,0},{2,1},{3,2},{4,3},{5,4},{6,5},{7,6},{8,7},{9,8},{10,9},{11,1... | collective-permute-start | bytes 4616 | tf_op jit(solution)/shard_map/ppermute | solution.py:28
  433.3 34.3 %copy-start.5 = (bf16[256,768]{1,0:T(8,128)(2,1)S(1)}, bf16[256,768]{1,0:T(8,128)(2,1)}, u32[]{:S(2)}) copy-start(bf16[256,768]{1,0:T(8,128)(2,1)} %reduce-scatter.8.cloned.1.call-done) | copy-start | bytes 1179652
  433.3 34.3 %collective-permute-start.6 = (bf16[1,768]{1,0:T(2,128)(2,1)S(1)}, bf16[1,768]{1,0:T(2,128)(2,1)S(1)}, u32[]{:S(2)}, u32[]{:S(2)}) collective-permute-start(bf16[1,768]{1,0:T(2,128)(2,1)S(1)} %get-tuple-element.16), channel_id=1, source_target_pairs={{0,1},{1,2},{2,3},{3,4},{4,5},{5,6},{6,7},{7,8},{8,9},{9,10},{10,1... | collective-permute-start | bytes 4616 | tf_op jit(solution)/shard_map/ppermute | solution.py:26
  465.8 4.4 copy-start.1
Sparse Core Ops, SparseCore 0:
  9.8 40.3 all-gather.4
  68.5 64.4 reduce-scatter.3
  135.5 38.2 all-gather.6
  179.1 63.4 reduce-scatter.5
  301.8 80.2 reduce-scatter.7
  383.7 39.4 all-gather.8
  425.1 38.8 all-gather.10
where the time goes:
time: 478 us; the launch traced here: 477 us
  waiting for transfers between devices  349 us (73%)
  matrix products  35.1 us (7%)
  local copies, waits for them, and re-layouts  23.1 us (5%)
  starting transfers between devices  22.8 us (5%)
  blocking collectives  21.4 us (4%)
  between operations  14.7 us (3%)
  other arithmetic  11.1 us (2%)
    reduce_scatter x1, waiting for transfers between devices, body(): lax.psum_scatter(phase_terms(prelude, w_upsample, jnp.int32(0) // 4, samp...  78 us
    reduce_scatter x1, waiting for transfers between devices, body(): lax.psum_scatter(jnp.dot(heads_out, w_heads_out, preferred_element_type=j...  64.6 us
    reduce_scatter x1, waiting for transfers between devices, body(): lax.psum_scatter(jnp.dot(hidden, w_down, preferred_element_type=jnp.float...  62.5 us
    all_gather x1, waiting for transfers between devices, body(): gathered = lax.all_gather(frames, 'sub', axis=0, tiled=True)  41.1 us
    all_gather x1, waiting for transfers between devices, body(): second_norm = lax.all_gather(own_norm, 'sub', axis=0, tiled=True)  38.8 us
    all_gather x1, waiting for transfers between devices, dilated_conv(): weight_rows = lax.all_gather(w_dilated, 'sub', axis=1, tiled=True)  32 us
    all_gather x1, waiting for transfers between devices, plain_conv(): weight_rows = lax.all_gather(w_plain, 'sub', axis=1, tiled=True)  27.2 us
    all_gather x1, blocking collectives, body(): mel_next = lax.all_gather(mel_own, 'sub', axis=0, tiled=True)  21.4 us
  transfers between devices with their start and end apart: 15, of which 8 were waited for; matrix products, arithmetic and copies ran while one was open for 4% of the time, Pallas kernels for 0%

commit v1 on v0

--- a/solution.py
+++ b/solution.py
@@ -114,7 +114,9 @@
 def plain_conv(extended, row_count, w_plain):
     empty_sum = jnp.zeros((row_count, w_plain.shape[2]), jnp.float32)
     running = empty_sum
-    weight_rows = lax.all_gather(w_plain, "sub", axis=1, tiled=True)
+    weight_rows = jnp.concatenate(
+        lax.all_to_all(jnp.stack([w_plain] * lax.axis_size("sub")), "sub", 0, 0), axis=1
+    )
     for offset in range(3):
         running = running + jnp.dot(
             extended[offset : offset + row_count],

time: 478 us -> 497 us (1.040); the launches traced: 477 us -> 489 us
  starting transfers between devices: 22.8 us -> 27.8 us
    all_to_all x0 -> x1, waiting for transfers between devices: none -> 51.5 us  [plain_conv(): lax.all_to_all(jnp.stack([w_plain] * lax.axis_size('sub')), 'sub', 0, 0)]
    all_gather x1 -> x0, waiting for transfers between devices: 27.2 us -> none  [plain_conv(): weight_rows = lax.all_gather(w_plain, 'sub', axis=1, tiled=True)]
    reduce_scatter x1, waiting for transfers between devices: 78 us -> 54 us  [body(): lax.psum_scatter(phase_terms(prelude, w_upsample, jnp.int32(0) // 4, samp...]
    all_to_all x0 -> x1, starting transfers between devices: none -> 5.26 us  [plain_conv(): lax.all_to_all(jnp.stack([w_plain] * lax.axis_size('sub')), 'sub', 0, 0)]
  transfers between devices with their start and end apart: 15 -> 15, of which waited for: 8 -> 9; matrix products, arithmetic and copies ran while one was open for 4% -> 4% of each run, Pallas kernels for 0% -> 0%
where the time goes in v1:
time: 497 us; the launch traced here: 489 us
  waiting for transfers between devices  353 us (71%)
  matrix products  31.3 us (6%)
  starting transfers between devices  27.8 us (6%)
  local copies, waits for them, and re-layouts  27.7 us (6%)
  blocking collectives  22.9 us (5%)
  between operations  14.7 us (3%)
  other arithmetic  12.1 us (2%)
    reduce_scatter x1, waiting for transfers between devices, body(): lax.psum_scatter(jnp.dot(heads_out, w_heads_out, preferred_element_type=j...  64.6 us
    reduce_scatter x1, waiting for transfers between devices, body(): lax.psum_scatter(jnp.dot(hidden, w_down, preferred_element_type=jnp.float...  62.5 us
    reduce_scatter x1, waiting for transfers between devices, body(): lax.psum_scatter(phase_terms(prelude, w_upsample, jnp.int32(0) // 4, samp...  54 us
    all_to_all x1, waiting for transfers between devices, plain_conv(): lax.all_to_all(jnp.stack([w_plain] * lax.axis_size('sub')), 'sub', 0, 0)  51.5 us
    all_gather x1, waiting for transfers between devices, body(): gathered = lax.all_gather(frames, 'sub', axis=0, tiled=True)  41.1 us
    all_gather x1, waiting for transfers between devices, body(): second_norm = lax.all_gather(own_norm, 'sub', axis=0, tiled=True)  38.8 us
    all_gather x1, waiting for transfers between devices, dilated_conv(): weight_rows = lax.all_gather(w_dilated, 'sub', axis=1, tiled=True)  35.8 us
    all_gather x1, blocking collectives, body(): mel_next = lax.all_gather(mel_own, 'sub', axis=0, tiled=True)  22.9 us
  transfers between devices with their start and end apart: 15, of which 9 were waited for; matrix products, arithmetic and copies ran while one was open for 4% of the time, Pallas kernels for 0%

profile of v1, /device:TPU:1, one launch (start us, length us, event | category | flops | bytes accessed | tf_op | source)
XLA Modules:
  0.0 489.0 jit_solution(1018895861501357432)
XLA Ops:
  7.2 0.7 all-gather.4.cloned.1.call-update
  8.1 1.1 slice_add_fusion
  9.2 41.1 %all-gather.4.cloned.1.call-done = bf16[1024,1024]{1,0:T(8,128)(2,1)} async-done(((bf16[64,1024]{1,0:T(8,128)(2,1)}), bf16[1024,1024]{1,0:T(8,128)(2,1)}) %all-gather.4.cloned.1.call-update) | async-done | bytes 2097168 | tf_op jit(solution)/shard_map/all_gather | solution.py:147
  50.2 2.4 convert_reduce_fusion
  52.7 2.2 fusion.14
  55.0 3.2 collective-permute-start.1
  58.6 3.2 collective-permute-start
  61.8 2.2 fusion.181
  64.0 2.1 fusion.27
  66.3 2.1 convolution_convert_fusion.1
  68.5 64.6 %reduce-scatter.4.cloned.1.call-done = bf16[64,1024]{1,0:T(8,128)(2,1)} async-done(((bf16[1024,1024]{1,0:T(8,128)(2,1)}), bf16[64,1024]{1,0:T(8,128)(2,1)}) %reduce-scatter.4.cloned.1.call-update) | async-done | bytes 131088 | tf_op jit(solution)/shard_map/reduce_scatter | solution.py:157
  133.1 1.1 convert_reduce_fusion.1
  134.2 0.8 fusion.83
  135.0 38.8 %all-gather.6.cloned.1.call-done = bf16[1024,1024]{1,0:T(8,128)(2,1)} async-done(((bf16[64,1024]{1,0:T(8,128)(2,1)}), bf16[1024,1024]{1,0:T(8,128)(2,1)}) %all-gather.6.cloned.1.call-update) | async-done | bytes 2097168 | tf_op jit(solution)/shard_map/all_gather | solution.py:165
  173.8 5.2 %convolution_convert_fusion = bf16[1024,1024]{1,0:T(8,128)(2,1)} fusion(bf16[256,1024]{1,0:T(8,128)(2,1)S(1)} %copy-done, bf16[1024,1024]{1,0:T(8,128)(2,1)} %all-gather.6.cloned.1.call-done, bf16[1024,256]{1,0:T(8,128)(2,1)S(1)} %copy-done.13), kind=kOutput, calls=%fused_computation.27 | convolution fusion | flops 1077149696 | bytes 5242880 | tf_op jit(solution)/shard_map/dot_general | solution.py:170
  179.1 1.0 constant_dynamic-slice_fusion
  180.2 62.5 %reduce-scatter.6.cloned.1.call-done = bf16[64,1024]{1,0:T(8,128)(2,1)} async-done(((bf16[1024,1024]{1,0:T(8,128)(2,1)}), bf16[64,1024]{1,0:T(8,128)(2,1)}) %reduce-scatter.6.cloned.1.call-update) | async-done | bytes 131088 | tf_op jit(solution)/shard_map/reduce_scatter | solution.py:169
  242.6 1.1 convert_reduce_fusion.2
  243.7 0.2 fusion.28
  244.0 22.9 %all_gather.14 = f32[1024,100]{1,0:T(8,128)} all-gather(f32[64,100]{1,0:T(8,128)S(1)} %fusion.28), channel_id=1, replica_groups=mesh['tm'=16,'sub'=16] {'sub'}, dimensions={0}, use_global_device_ids=true | all-gather | bytes 435200 | tf_op jit(solution)/shard_map/all_gather | solution.py:180
  266.9 1.1 convert_element_type.109
  268.0 3.2 collective-permute-start.2
  271.1 1.5 collective-permute-start.3
  272.6 2.8 collective-permute-done.3
  275.5 0.7 concatenate.44
  276.2 0.2 fusion.69
  276.4 0.2 fusion.61
  276.7 0.2 fusion.71
  276.9 0.2 fusion.58
  277.2 0.2 fusion.55
  277.4 0.2 fusion.65
  277.7 0.3 fusion.13
  278.0 0.7 copy-done.7
  278.7 0.7 fusion.113
  279.4 0.7 fusion.110
  280.1 0.7 fusion.107
  280.9 0.7 fusion.104
  281.6 0.6 fusion.17
  282.2 0.6 fusion.18
  282.8 0.7 fusion.19
  283.5 0.7 fusion.20
  284.3 0.8 pad_maximum_fusion
  285.1 7.5 %copy.33 = bf16[1024,4,768]{2,1,0:T(4,128)(2,1)} copy(bf16[1024,4,768]{2,0,1:T(8,128)(2,1)S(1)} %pad_maximum_fusion) | data formatting | bytes 12582912 | tf_op jit(solution)/shard_map/stack | solution.py:61
  292.6 10.7 %convert_element_type.111 = bf16[4096,768]{1,0:T(8,128)(2,1)} reshape(bf16[1024,4,768]{2,1,0:T(4,128)(2,1)} %copy.33) | data formatting | bytes 12582912 | tf_op jit(solution)/shard_map/convert_element_type | solution.py:199
  303.4 0.5 all-gather.8.cloned.1.call-update
  303.9 0.3 copy-done.9
  304.3 2.1 stack.44
  306.4 5.3 %all-to-all-start = ((bf16[16,3,48,768]{3,2,1,0:T(8,128)(2,1)}), bf16[16,3,48,768]{3,2,1,0:T(8,128)(2,1)S(1)}, u32[]{:S(2)}, u32[]{:S(2)}) async-start(bf16[16,3,48,768]{3,2,1,0:T(8,128)(2,1)} %stack.44), calls=%async_computation.3 | async-start | bytes 7077888 | tf_op jit(solution)/shard_map/all_to_all | solution.py:118
  311.6 51.5 %all-to-all-done = bf16[16,3,48,768]{3,2,1,0:T(8,128)(2,1)S(1)} async-done(((bf16[16,3,48,768]{3,2,1,0:T(8,128)(2,1)}), bf16[16,3,48,768]{3,2,1,0:T(8,128)(2,1)S(1)}, u32[]{:S(2)}, u32[]{:S(2)}) %all-to-all-start) | async-done | bytes 3538976 | tf_op jit(solution)/shard_map/all_to_all | solution.py:118
  363.2 1.9 fusion.175
  365.0 2.0 copy.34
  367.1 54.0 %reduce-scatter.8.cloned.1.call-done = bf16[256,768]{1,0:T(8,128)(2,1)} async-done(((bf16[4096,768]{1,0:T(8,128)(2,1)}), bf16[256,768]{1,0:T(8,128)(2,1)}) %reduce-scatter.8.cloned.1.call-update) | async-done | bytes 393232 | tf_op jit(solution)/shard_map/reduce_scatter | solution.py:196
  421.0 3.6 fusion.43
  424.7 3.2 collective-permute-start.5
  427.9 2.4 collective-permute-start.4
  430.3 35.8 %all-gather.8.cloned.1.call-done = bf16[3,768,768]{2,1,0:T(8,128)(2,1)} async-done(((bf16[3,48,768]{2,1,0:T(8,128)(2,1)}), bf16[3,768,768]{2,1,0:T(8,128)(2,1)}) %all-gather.8.cloned.1.call-update) | async-done | bytes 3538960 | tf_op jit(solution)/shard_map/all_gather | solution.py:104
  466.1 1.7 fusion.26
  467.8 1.8 fusion.25
  469.6 4.3 add_convert_fusion.4
  474.0 2.3 collective-permute-start.7
  476.4 0.5 fusion.186
  476.8 3.4 collective-permute-start.6
  480.3 0.5 fusion.49
  480.9 1.2 fusion.24
  (72 shorter events, 1.5 us)
Async XLA Ops:
  7.2 166.7 %copy-start = (bf16[256,1024]{1,0:T(8,128)(2,1)S(1)}, bf16[256,1024]{1,0:T(8,128)(2,1)}, u32[]{:S(2)}) copy-start(bf16[256,1024]{1,0:T(8,128)(2,1)} %param.18) | copy-start | bytes 1572868
  7.2 43.1 %all-gather.4.cloned.1.call-start = ((), (), s32[]{:S(2)}) async-start(), calls=%async_computation.4 | async-start | bytes 2228224 | tf_op jit(solution)/shard_map/all_gather | solution.py:147
  7.9 125.2 %reduce-scatter.4.cloned.1.call-start = ((), (), s32[]{:S(2)}) async-start(), calls=%async_computation.5 | async-start | bytes 2228224 | tf_op jit(solution)/shard_map/reduce_scatter | solution.py:157
  50.2 2.4 copy-start.5
  55.0 6.8 %collective-permute-start.1 = (bf16[256,64]{0,1:T(8,128)(2,1)S(1)}, bf16[256,64]{0,1:T(8,128)(2,1)S(1)}, u32[]{:S(2)}, u32[]{:S(2)}) collective-permute-start(bf16[256,64]{0,1:T(8,128)(2,1)S(1)} %get-tuple-element.24), channel_id=1, source_target_pairs={{0,16},{16,32},{32,48},{48,64},{64,80},{80,96},{96,112},{112,128},... | collective-permute-start | bytes 98312 | tf_op jit(solution)/shard_map/ppermute | solution.py:15
  58.6 5.4 %collective-permute-start = (bf16[256,64]{0,1:T(8,128)(2,1)S(1)}, bf16[256,64]{0,1:T(8,128)(2,1)S(1)}, u32[]{:S(2)}, u32[]{:S(2)}) collective-permute-start(bf16[256,64]{0,1:T(8,128)(2,1)S(1)} %get-tuple-element.23), channel_id=1, source_target_pairs={{0,16},{16,32},{32,48},{48,64},{64,80},{80,96},{96,112},{112,128},... | collective-permute-start | bytes 98312 | tf_op jit(solution)/shard_map/ppermute | solution.py:15
  64.0 2.3 copy-start.11
  66.3 66.8 %copy-start.8 = (bf16[64,1024]{1,0:T(8,128)(2,1)S(1)}, bf16[64,1024]{1,0:T(8,128)(2,1)}, u32[]{:S(2)}) copy-start(bf16[64,1024]{1,0:T(8,128)(2,1)} %param.13) | copy-start | bytes 393220
  66.3 107.5 %copy-start.13 = (bf16[1024,256]{1,0:T(8,128)(2,1)S(1)}, bf16[1024,256]{1,0:T(8,128)(2,1)}, u32[]{:S(2)}) copy-start(bf16[1024,256]{1,0:T(8,128)(2,1)} %param.17) | copy-start | bytes 1572868
  68.4 105.4 %all-gather.6.cloned.1.call-start = ((), (), s32[]{:S(2)}) async-start(), calls=%async_computation.6 | async-start | bytes 2228224 | tf_op jit(solution)/shard_map/all_gather | solution.py:165
  135.0 107.7 %reduce-scatter.6.cloned.1.call-start = ((), (), s32[]{:S(2)}) async-start(), calls=%async_computation.7 | async-start | bytes 2228224 | tf_op jit(solution)/shard_map/reduce_scatter | solution.py:169
  179.0 64.7 %copy-start.14 = (bf16[1024,100]{0,1:T(8,128)(2,1)S(1)}, bf16[1024,100]{0,1:T(8,128)(2,1)}, u32[]{:S(2)}) copy-start(bf16[1024,100]{0,1:T(8,128)(2,1)} %param.19) | copy-start | bytes 614404
  179.0 97.2 %copy-start.10 = (bf16[7,96,100]{2,1,0:T(8,128)(2,1)S(1)}, bf16[7,96,100]{2,1,0:T(8,128)(2,1)}, u32[]{:S(2)}) copy-start(bf16[7,96,100]{2,1,0:T(8,128)(2,1)} %param.21) | copy-start | bytes 403204
  179.0 242.0 %reduce-scatter.8.cloned.1.call-start = ((), (), s32[]{:S(2)}) async-start(), calls=%async_computation.8 | async-start | bytes 6684672 | tf_op jit(solution)/shard_map/reduce_scatter | solution.py:196
  268.0 4.7 collective-permute-start.2
  271.1 4.3 collective-permute-start.3
  277.4 1.3 copy-start.7
  303.3 0.9 copy-start.9
  303.3 162.7 %all-gather.8.cloned.1.call-start = ((), (), s32[]{:S(2)}) async-start(), calls=%async_computation.9 | async-start | bytes 3760128 | tf_op jit(solution)/shard_map/all_gather | solution.py:104
  306.4 5.3 %copy-start.12 = (f32[2,768]{1,0:T(2,128)S(1)}, f32[2,768]{1,0:T(2,128)}, u32[]{:S(2)}) copy-start(f32[2,768]{1,0:T(2,128)} %param.23) | copy-start | bytes 18436
  306.4 56.8 %all-to-all-start = ((bf16[16,3,48,768]{3,2,1,0:T(8,128)(2,1)}), bf16[16,3,48,768]{3,2,1,0:T(8,128)(2,1)S(1)}, u32[]{:S(2)}, u32[]{:S(2)}) async-start(bf16[16,3,48,768]{3,2,1,0:T(8,128)(2,1)} %stack.44), calls=%async_computation.3 | async-start | bytes 7077888 | tf_op jit(solution)/shard_map/all_to_all | solution.py:118
  424.7 43.1 %collective-permute-start.5 = (bf16[3,768]{1,0:T(4,128)(2,1)S(1)}, bf16[3,768]{1,0:T(4,128)(2,1)S(1)}, u32[]{:S(2)}, u32[]{:S(2)}) collective-permute-start(bf16[3,768]{1,0:T(4,128)(2,1)S(1)} %get-tuple-element.22), channel_id=1, source_target_pairs={{1,0},{2,1},{3,2},{4,3},{5,4},{6,5},{7,6},{8,7},{9,8},{10,9},{11,1... | collective-permute-start | bytes 13832 | tf_op jit(solution)/shard_map/ppermute | solution.py:28
  427.9 41.7 %collective-permute-start.4 = (bf16[3,768]{1,0:T(4,128)(2,1)S(1)}, bf16[3,768]{1,0:T(4,128)(2,1)S(1)}, u32[]{:S(2)}, u32[]{:S(2)}) collective-permute-start(bf16[3,768]{1,0:T(4,128)(2,1)S(1)} %get-tuple-element.21), channel_id=1, source_target_pairs={{0,1},{1,2},{2,3},{3,4},{4,5},{5,6},{6,7},{7,8},{8,9},{9,10},{10,1... | collective-permute-start | bytes 13832 | tf_op jit(solution)/shard_map/ppermute | solution.py:26
  469.6 6.7 %copy-start.3 = (bf16[1,16,48,768]{3,2,0,1:T(8,128)(2,1)S(1)}, bf16[1,16,48,768]{3,2,0,1:T(8,128)(2,1)}, u32[]{:S(2)}) copy-start(bf16[1,16,48,768]{3,2,0,1:T(8,128)(2,1)} %get-tuple-element.18) | copy-start | bytes 3538948
  474.0 6.3 %copy-start.2 = (bf16[1,16,48,768]{3,2,0,1:T(8,128)(2,1)S(1)}, bf16[1,16,48,768]{3,2,0,1:T(8,128)(2,1)}, u32[]{:S(2)}) copy-start(bf16[1,16,48,768]{3,2,0,1:T(8,128)(2,1)} %get-tuple-element.17) | copy-start | bytes 3538948
  474.0 6.2 %collective-permute-start.7 = (bf16[1,768]{1,0:T(2,128)(2,1)S(1)}, bf16[1,768]{1,0:T(2,128)(2,1)S(1)}, u32[]{:S(2)}, u32[]{:S(2)}) collective-permute-start(bf16[1,768]{1,0:T(2,128)(2,1)S(1)} %get-tuple-element.20), channel_id=1, source_target_pairs={{1,0},{2,1},{3,2},{4,3},{5,4},{6,5},{7,6},{8,7},{9,8},{10,9},{11,1... | collective-permute-start | bytes 4616 | tf_op jit(solution)/shard_map/ppermute | solution.py:28
  476.3 4.6 copy-start.4
  476.4 4.6 copy-start.6
  476.8 4.1 collective-permute-start.6
  480.2 1.9 copy-start.1
Sparse Core Ops, SparseCore 0:
  9.8 40.3 all-gather.3
  68.5 64.4 reduce-scatter.3
  135.5 38.2 all-gather.5
  179.2 63.4 reduce-scatter.5
  303.5 117.5 reduce-scatter.7
  422.7 43.3 all-gather.7
